TPU v7x, 128 devices: a whole 4x4x4 slice. The times are simulated.
128 devices in a mesh: cells: 128 (over z, x, y, core).
Axes of the slice: x: 4, y: 4, z: 4, core: 2. Of those that a mesh axis runs over, the one named last changes fastest.
Arguments:
- channels: float32 [256, 41, 64, 128], P('cells'), may hold values from -0.44194174 to 0.44194174, as said below
- precoders_init: float32 [256, 16, 128], P('cells'), may hold values from -1 to 1
- receiver_cells: int32 [256], replicated, may hold values from 0 to 255, as said below
- transmitter_cells: int32 [256], replicated, may hold values from 0 to 255, as said below
- interferers: int32 [256, 40], replicated, may hold values from 0 to 255, as said below
- counts: int32 [256], replicated, may hold values from 24 to 40
Outputs:
- precoders: float32 [256, 16, 128], P('cells')
- mse_weights: float32 [256, 256], P('cells')
Inputs may be any that keep to these rules, and one draw needn't show every extreme that they name: `receiver_cells`: A permutation of the cells; receiver slots s lie on device s // 2. `transmitter_cells`: A permutation of the cells; transmitter slots t lie on device t // 2. `interferers`: each row holds distinct cells, never the cell of its own receiver slot. Over the receiver slots of one device, the links in use (own links included) whose transmitter slot lies on any one device number at most 1, and 1 is reached in every draw. `channels`: own links (m = 0) are drawn stronger than interfering ones.
All inputs are finite; a program needn't handle non-finite values.
Results may differ from a plain program's by a relative error of at most 0.0003.
Values sent between devices are 32-bit elements; how exact they have to be, the bound alone decides.
A program may use at most 64 MiB of HBM per device.

v0:
```python
import jax
import jax.numpy as jnp
from jax import lax
from jax.sharding import PartitionSpec as P

LAYERS = 4
NOISE_POWER = 1.0
STEP_SIZES = (0.3, 0.2, 0.15, 0.1)
HIGHEST = lax.Precision.HIGHEST


def spd_solve(matrix, right_side):
    factor = jnp.linalg.cholesky(matrix)
    middle = lax.linalg.triangular_solve(factor, right_side, left_side=True, lower=True)
    return lax.linalg.triangular_solve(factor, middle, left_side=True, lower=True, transpose_a=True)


def link_tables(receiver_cells, transmitter_cells, interferers, counts):
    inverse = jnp.argsort(transmitter_cells)
    linked = jnp.concatenate([receiver_cells[:, None], interferers], axis=1)
    positions = inverse[linked]
    in_use = jnp.arange(interferers.shape[1] + 1, dtype=jnp.int32)[None, :] <= counts[:, None]
    return (positions, in_use)


def receiver_step(channels, link_precoders, in_use):
    weight_mask = in_use.astype(jnp.float32)
    images = jnp.einsum("klrn,kldn->kldr", channels, link_precoders, precision=HIGHEST)
    masked = images * weight_mask[:, :, None, None]
    receive_size = channels.shape[2]
    stream_count = link_precoders.shape[2]
    covariance = jnp.einsum(
        "kldr,klds->krs", masked, images, precision=HIGHEST
    ) + NOISE_POWER * jnp.eye(receive_size, dtype=jnp.float32)
    direct = images[:, 0]
    filters = spd_solve(covariance, jnp.swapaxes(direct, 1, 2))
    identity = jnp.eye(stream_count, dtype=jnp.float32)
    errors = identity - jnp.einsum("krd,ker->kde", filters, direct, precision=HIGHEST)
    weights = spd_solve(errors, jnp.broadcast_to(identity, errors.shape))
    transposed = (
        jnp.einsum("krd,klrn->kldn", filters, channels, precision=HIGHEST)
        * weight_mask[:, :, None, None]
    )
    return (weights, transposed)


def body(channels, precoders_init, receiver_cells, transmitter_cells, interferers, counts):
    devices = lax.axis_size("cells")
    own_index = lax.axis_index("cells")
    groups = channels.shape[0]
    link_count = channels.shape[1]
    streams = precoders_init.shape[1]
    antennas = precoders_init.shape[2]
    per_device = groups * link_count
    capacity = (per_device + devices - 1) // devices
    slot_total = devices * capacity
    positions, in_use = link_tables(receiver_cells, transmitter_cells, interferers, counts)
    device_of = (positions // groups).reshape(devices, per_device)
    local_of = (positions % groups).reshape(devices, per_device)
    in_service = in_use.reshape(devices, per_device)
    position_index = jnp.arange(per_device, dtype=jnp.int32)
    arriving = in_service & (device_of == own_index)
    ranked = jnp.cumsum(arriving.astype(jnp.int32), axis=1) - 1
    picker = arriving[:, None, :] & (
        ranked[:, None, :] == jnp.arange(capacity, dtype=jnp.int32)[None, :, None]
    )
    slot_used = jnp.any(picker, axis=2).reshape(-1)
    slot_local = jnp.sum(picker * local_of[:, None, :], axis=2).reshape(-1)
    slot_direct = jnp.any(
        picker & (position_index % link_count == 0)[None, None, :], axis=2
    ).reshape(-1)
    mine_device = device_of[own_index]
    mine_service = in_service[own_index]
    mine_positions = positions.reshape(devices, per_device)[own_index]
    earlier = (
        mine_service[None, :]
        & (mine_device[None, :] == mine_device[:, None])
        & (position_index[None, :] < position_index[:, None])
    )
    mine_rank = jnp.sum(earlier.astype(jnp.int32), axis=1)
    mine_index = jnp.where(mine_service, mine_device * capacity + mine_rank, 0)
    back_pick = mine_service[None, :] & (
        mine_index[None, :] == jnp.arange(slot_total, dtype=jnp.int32)[:, None]
    )
    back_used = jnp.any(back_pick, axis=1).astype(jnp.float32)
    back_position = jnp.sum(back_pick * position_index[None, :], axis=1)
    my_in_use = in_use.reshape(devices, groups, link_count)[own_index]
    target_mask = (
        (slot_local[None, :] == jnp.arange(groups, dtype=jnp.int32)[:, None]) & slot_used[None, :]
    ).astype(jnp.float32)
    direct_mask = target_mask * slot_direct.astype(jnp.float32)[None, :]
    precoders = precoders_init
    weights = jnp.zeros((groups, streams, streams), jnp.float32)
    for layer_index in range(LAYERS):
        everything = lax.all_gather(precoders, "cells", axis=0, tiled=True)
        link_precoders = everything[mine_positions]
        weights, transposed = receiver_step(
            channels, link_precoders.reshape(groups, link_count, streams, antennas), my_in_use
        )
        flat_filters = transposed.reshape(per_device, streams, antennas)
        outgoing_filters = (flat_filters[back_position] * back_used[:, None, None]).reshape(
            devices, capacity, streams, antennas
        )
        link_weights = (
            weights.reshape(groups, streams * streams)[back_position // link_count]
            * back_used[:, None]
        )
        arrived, arrived_weights = (
            lax.all_to_all(outgoing_filters, "cells", split_axis=0, concat_axis=0, tiled=True),
            lax.all_to_all(
                link_weights.reshape(devices, capacity, streams * streams),
                "cells",
                split_axis=0,
                concat_axis=0,
                tiled=True,
            ),
        )
        arrived_weights = arrived_weights.reshape(slot_total, streams, streams)
        arrived = arrived.reshape(slot_total, streams, antennas)
        weighted = jnp.einsum("sed,sen->sdn", arrived_weights, arrived, precision=HIGHEST)
        selected = target_mask[:, :, None, None] * arrived[None]
        system = jnp.einsum("gsdn,sdm->gnm", selected, weighted, precision=HIGHEST)
        system = system + STEP_SIZES[layer_index] * jnp.eye(antennas, dtype=jnp.float32)
        right_side = jnp.einsum("gs,sdn->gdn", direct_mask, weighted, precision=HIGHEST)
        precoders = jnp.swapaxes(spd_solve(system, jnp.swapaxes(right_side, 1, 2)), 1, 2)
    return (precoders, weights.reshape(groups, streams * streams))


def solution(mesh):
    return jax.shard_map(
        body,
        mesh=mesh,
        in_specs=(P("cells", None, None, None), P("cells", None, None), P(), P(), P(), P()),
        out_specs=(P("cells", None, None), P("cells", None)),
        check_vma=False,
    )
```

profile of v0, /device:TPU:1, one launch (start us, length us, event | category | flops | bytes accessed | tf_op | source)
XLA Modules:
  0.0 852.8 jit_solution(2282363171503754856)
XLA Ops:
  13.8 61.3 %gather_fusion = s32[10496]{0:T(1024)S(1)} fusion(s32[256]{0:T(256)S(1)} %get-tuple-element.6, s32[11264]{0:T(1024)S(1)} %pad_clamp_fusion), kind=kCustom, calls=%fused_computation | custom fusion | bytes 125952 | tf_op jit(solution)/shard_map/gather | solution.py:21
  83.4 5.4 broadcast_multiply_fusion.3
  92.7 12.5 %custom-call.54 = f32[2,64,64]{2,1,0:T(8,128)S(1)} custom-call(f32[2,64,64]{2,1,0:T(8,128)} %fusion.99), custom_call_target="Cholesky" | custom-call | tf_op jit(solution)/shard_map/jit(cholesky)/cholesky | solution.py:13
  106.0 10.6 %custom-call.56 = f32[2,1,64,64]{2,3,1,0:T(8,128)S(1)} custom-call(f32[2,1,64,64]{3,2,1,0:T(8,128)} %select_bitcast_fusion.7), custom_call_target="InvertDiagBlocksLowerTriangular" | custom-call | tf_op jit(solution)/shard_map/triangular_solve/custom-call.4 | solution.py:15
  130.1 12.0 %all-to-all-start.1 = ((f32[128,1,256]{2,1,0:T(1,128)}), f32[128,1,256]{2,1,0:T(1,128)}, u32[]{:S(2)}, u32[]{:S(2)}) async-start(f32[128,1,256]{2,1,0:T(1,128)} %copy.284), calls=%async_computation.1 | async-start | bytes 262144 | tf_op jit(solution)/shard_map/all_to_all | solution.py:110
  160.2 15.4 %all-to-all-done = f32[128,1,16,128]{3,2,1,0:T(8,128)} async-done(((f32[128,1,16,128]{3,2,1,0:T(8,128)}), f32[128,1,16,128]{3,2,1,0:T(8,128)}, u32[]{:S(2)}, u32[]{:S(2)}) %all-to-all-start) | async-done | bytes 1048608 | tf_op jit(solution)/shard_map/all_to_all | solution.py:109
  184.3 23.5 %custom-call.60 = f32[2,128,128]{2,1,0:T(8,128)S(1)} custom-call(f32[2,128,128]{2,1,0:T(8,128)S(1)} %fusion.79), custom_call_target="Cholesky" | custom-call | tf_op jit(solution)/shard_map/jit(cholesky)/cholesky | solution.py:13
  208.0 19.7 %custom-call.62 = f32[2,1,128,128]{2,3,1,0:T(8,128)S(1)} custom-call(f32[2,1,128,128]{3,2,1,0:T(8,128)S(1)} %select_bitcast_fusion.3), custom_call_target="InvertDiagBlocksLowerTriangular" | custom-call | tf_op jit(solution)/shard_map/triangular_solve/custom-call.8 | solution.py:15
  230.9 62.4 %all-gather.7.cloned.1.call-done = f32[256,16,128]{2,1,0:T(8,128)} async-done(((f32[2,16,128]{2,1,0:T(8,128)}), f32[256,16,128]{2,1,0:T(8,128)}) %all-gather.7.cloned.1.call-update) | async-done | bytes 2097168 | tf_op jit(solution)/shard_map/all_gather | solution.py:95
  296.5 5.4 broadcast_multiply_fusion.2
  305.9 12.6 %custom-call.63 = f32[2,64,64]{2,1,0:T(8,128)S(1)} custom-call(f32[2,64,64]{2,1,0:T(8,128)} %fusion.94), custom_call_target="Cholesky" | custom-call | tf_op jit(solution)/shard_map/jit(cholesky)/cholesky | solution.py:13
  319.3 10.6 %custom-call.65 = f32[2,1,64,64]{2,3,1,0:T(8,128)S(1)} custom-call(f32[2,1,64,64]{3,2,1,0:T(8,128)} %select_bitcast_fusion.6), custom_call_target="InvertDiagBlocksLowerTriangular" | custom-call | tf_op jit(solution)/shard_map/triangular_solve/custom-call.4 | solution.py:15
  342.7 5.8 all-to-all-start.3
  352.8 5.5 all-to-all-done.3
  366.1 16.0 %all-to-all-done.2 = f32[128,1,16,128]{3,2,1,0:T(8,128)} async-done(((f32[128,1,16,128]{3,2,1,0:T(8,128)}), f32[128,1,16,128]{3,2,1,0:T(8,128)}, u32[]{:S(2)}, u32[]{:S(2)}) %all-to-all-start.2) | async-done | bytes 1048608 | tf_op jit(solution)/shard_map/all_to_all | solution.py:109
  393.0 23.7 %custom-call.69 = f32[2,128,128]{2,1,0:T(8,128)S(1)} custom-call(f32[2,128,128]{2,1,0:T(8,128)S(1)} %fusion.75), custom_call_target="Cholesky" | custom-call | tf_op jit(solution)/shard_map/jit(cholesky)/cholesky | solution.py:13
  416.9 19.7 %custom-call.71 = f32[2,1,128,128]{2,3,1,0:T(8,128)S(1)} custom-call(f32[2,1,128,128]{3,2,1,0:T(8,128)S(1)} %select_bitcast_fusion.2), custom_call_target="InvertDiagBlocksLowerTriangular" | custom-call | tf_op jit(solution)/shard_map/triangular_solve/custom-call.8 | solution.py:15
  437.8 62.4 %all-gather.9.cloned.1.call-done = f32[256,16,128]{2,1,0:T(8,128)} async-done(((f32[2,16,128]{2,1,0:T(8,128)}), f32[256,16,128]{2,1,0:T(8,128)}) %all-gather.9.cloned.1.call-update) | async-done | bytes 2097168 | tf_op jit(solution)/shard_map/all_gather | solution.py:95
  512.7 12.9 %custom-call.72 = f32[2,64,64]{2,1,0:T(8,128)S(1)} custom-call(f32[2,64,64]{2,1,0:T(8,128)} %fusion.89), custom_call_target="Cholesky" | custom-call | tf_op jit(solution)/shard_map/jit(cholesky)/cholesky | solution.py:13
  526.4 10.6 %custom-call.74 = f32[2,1,64,64]{2,3,1,0:T(8,128)S(1)} custom-call(f32[2,1,64,64]{3,2,1,0:T(8,128)} %select_bitcast_fusion.5), custom_call_target="InvertDiagBlocksLowerTriangular" | custom-call | tf_op jit(solution)/shard_map/triangular_solve/custom-call.4 | solution.py:15
  548.5 5.8 all-to-all-start.5
  558.5 5.5 all-to-all-done.5
  571.8 16.0 %all-to-all-done.4 = f32[128,1,16,128]{3,2,1,0:T(8,128)} async-done(((f32[128,1,16,128]{3,2,1,0:T(8,128)}), f32[128,1,16,128]{3,2,1,0:T(8,128)}, u32[]{:S(2)}, u32[]{:S(2)}) %all-to-all-start.4) | async-done | bytes 1048608 | tf_op jit(solution)/shard_map/all_to_all | solution.py:109
  598.7 23.6 %custom-call.78 = f32[2,128,128]{2,1,0:T(8,128)S(1)} custom-call(f32[2,128,128]{2,1,0:T(8,128)S(1)} %fusion.71), custom_call_target="Cholesky" | custom-call | tf_op jit(solution)/shard_map/jit(cholesky)/cholesky | solution.py:13
  622.6 19.7 %custom-call.80 = f32[2,1,128,128]{2,3,1,0:T(8,128)S(1)} custom-call(f32[2,1,128,128]{3,2,1,0:T(8,128)S(1)} %select_bitcast_fusion.1), custom_call_target="InvertDiagBlocksLowerTriangular" | custom-call | tf_op jit(solution)/shard_map/triangular_solve/custom-call.8 | solution.py:15
  643.5 62.4 %all-gather.11.cloned.1.call-done = f32[256,16,128]{2,1,0:T(8,128)} async-done(((f32[2,16,128]{2,1,0:T(8,128)}), f32[256,16,128]{2,1,0:T(8,128)}) %all-gather.11.cloned.1.call-update) | async-done | bytes 2097168 | tf_op jit(solution)/shard_map/all_gather | solution.py:95
  716.9 12.5 %custom-call.81 = f32[2,64,64]{2,1,0:T(8,128)S(1)} custom-call(f32[2,64,64]{2,1,0:T(8,128)} %fusion.84), custom_call_target="Cholesky" | custom-call | tf_op jit(solution)/shard_map/jit(cholesky)/cholesky | solution.py:13
  730.3 9.8 %custom-call.83 = f32[2,1,64,64]{2,3,1,0:T(8,128)S(1)} custom-call(f32[2,1,64,64]{3,2,1,0:T(8,128)S(1)} %select_bitcast_fusion.4), custom_call_target="InvertDiagBlocksLowerTriangular" | custom-call | tf_op jit(solution)/shard_map/triangular_solve/custom-call.4 | solution.py:15
  761.0 5.6 all-to-all-done.7
  773.6 16.9 %all-to-all-done.6 = f32[128,1,16,128]{3,2,1,0:T(8,128)} async-done(((f32[128,1,16,128]{3,2,1,0:T(8,128)}), f32[128,1,16,128]{3,2,1,0:T(8,128)}, u32[]{:S(2)}, u32[]{:S(2)}) %all-to-all-start.6) | async-done | bytes 1048608 | tf_op jit(solution)/shard_map/all_to_all | solution.py:109
  801.3 23.5 %custom-call.87 = f32[2,128,128]{2,1,0:T(8,128)S(1)} custom-call(f32[2,128,128]{2,1,0:T(8,128)S(1)} %fusion.67), custom_call_target="Cholesky" | custom-call | tf_op jit(solution)/shard_map/jit(cholesky)/cholesky | solution.py:13
  825.0 19.7 %custom-call.89 = f32[2,1,128,128]{2,3,1,0:T(8,128)S(1)} custom-call(f32[2,1,128,128]{3,2,1,0:T(8,128)S(1)} %select_bitcast_fusion), custom_call_target="InvertDiagBlocksLowerTriangular" | custom-call | tf_op jit(solution)/shard_map/triangular_solve/custom-call.8 | solution.py:15
  (298 shorter events, 208.9 us)
Async XLA Ops:
  7.2 76.2 %copy-start = (f32[2,41,64,128]{3,2,1,0:T(8,128)S(1)}, f32[2,41,64,128]{3,2,1,0:T(8,128)}, u32[]{:S(2)}) copy-start(f32[2,41,64,128]{3,2,1,0:T(8,128)} %param.21) | copy-start | bytes 8060932
  7.2 73.1 %all-gather.5.cloned.1.call-start = ((), (), s32[]{:S(2)}) async-start(), calls=%async_computation.8 | async-start | bytes 2113536 | tf_op jit(solution)/shard_map/all_gather | solution.py:95
  78.9 26.2 %copy-start.10 = (pred[64,64]{1,0:T(8,128)(4,1)}, pred[64,64]{1,0:T(8,128)(4,1)S(1)}, u32[]{:S(2)}) copy-start(pred[64,64]{1,0:T(8,128)(4,1)S(1)} %iota_compare_fusion.6) | copy-start | bytes 12292
  79.8 37.2 %copy-start.13 = (f32[2,41]{1,0:T(2,128)}, f32[2,41]{1,0:T(2,128)S(1)}, u32[]{:S(2)}) copy-start(f32[2,41]{1,0:T(2,128)S(1)} %fusion.166) | copy-start | bytes 988
  88.7 28.0 %copy-start.7 = (f32[2,41,16,64]{3,2,1,0:T(8,128)}, f32[2,41,16,64]{3,2,1,0:T(8,128)S(1)}, u32[]{:S(2)}) copy-start(f32[2,41,16,64]{3,2,1,0:T(8,128)S(1)} %get-tuple-element.24) | copy-start | bytes 1007620
  130.1 21.8 %all-to-all-start.1 = ((f32[128,1,256]{2,1,0:T(1,128)}), f32[128,1,256]{2,1,0:T(1,128)}, u32[]{:S(2)}, u32[]{:S(2)}) async-start(f32[128,1,256]{2,1,0:T(1,128)} %copy.284), calls=%async_computation.1 | async-start | bytes 262144 | tf_op jit(solution)/shard_map/all_to_all | solution.py:110
  151.9 23.8 %all-to-all-start = ((f32[128,1,16,128]{3,2,1,0:T(8,128)}), f32[128,1,16,128]{3,2,1,0:T(8,128)}, u32[]{:S(2)}, u32[]{:S(2)}) async-start(f32[128,1,16,128]{3,2,1,0:T(8,128)} %bitcast_multiply_fusion.3), calls=%async_computation | async-start | bytes 2097152 | tf_op jit(solution)/shard_map/all_to_all | solution.py:109
  157.1 136.3 %all-gather.7.cloned.1.call-start = ((), (), s32[]{:S(2)}) async-start(), calls=%async_computation.9 | async-start | bytes 2113536 | tf_op jit(solution)/shard_map/all_gather | solution.py:95
  157.7 69.9 %copy-start.31 = (f32[128]{0:T(128)}, f32[128]{0:T(128)S(1)}, u32[]{:S(2)}) copy-start(f32[128]{0:T(128)S(1)} %convert_element_type.98) | copy-start | bytes 1540
  157.8 23.2 %copy-start.22 = (f32[2,128]{1,0:T(2,128)}, f32[2,128]{1,0:T(2,128)S(1)}, u32[]{:S(2)}) copy-start(f32[2,128]{1,0:T(2,128)S(1)} %get-tuple-element.12) | copy-start | bytes 3076
  157.8 69.8 %copy-start.26 = (pred[2,128]{1,0:T(4,128)(4,1)}, pred[2,128]{1,0:T(4,128)(4,1)S(1)}, u32[]{:S(2)}) copy-start(pred[2,128]{1,0:T(4,128)(4,1)S(1)} %get-tuple-element.14) | copy-start | bytes 772
  182.0 114.5 %copy-start.14 = (f32[2,41]{1,0:T(2,128)S(1)}, f32[2,41]{1,0:T(2,128)}, u32[]{:S(2)}) copy-start(f32[2,41]{1,0:T(2,128)} %copy-done.13) | copy-start | bytes 988
  342.7 15.6 %all-to-all-start.3 = ((f32[128,1,256]{2,1,0:T(1,128)}), f32[128,1,256]{2,1,0:T(1,128)}, u32[]{:S(2)}, u32[]{:S(2)}) async-start(f32[128,1,256]{2,1,0:T(1,128)} %copy.308), calls=%async_computation.3 | async-start | bytes 262144 | tf_op jit(solution)/shard_map/all_to_all | solution.py:110
  358.3 23.8 %all-to-all-start.2 = ((f32[128,1,16,128]{3,2,1,0:T(8,128)}), f32[128,1,16,128]{3,2,1,0:T(8,128)}, u32[]{:S(2)}, u32[]{:S(2)}) async-start(f32[128,1,16,128]{3,2,1,0:T(8,128)} %bitcast_multiply_fusion.2), calls=%async_computation.2 | async-start | bytes 2097152 | tf_op jit(solution)/shard_map/all_to_all | solution.py:109
  363.5 22.3 %copy-start.27 = (pred[2,128]{1,0:T(4,128)(4,1)S(1)}, pred[2,128]{1,0:T(4,128)(4,1)}, u32[]{:S(2)}) copy-start(pred[2,128]{1,0:T(4,128)(4,1)} %copy-done.26) | copy-start | bytes 772
  363.5 22.2 %copy-start.32 = (f32[128]{0:T(128)S(1)}, f32[128]{0:T(128)}, u32[]{:S(2)}) copy-start(f32[128]{0:T(128)} %copy-done.31) | copy-start | bytes 1540
  363.5 136.6 %all-gather.9.cloned.1.call-start = ((), (), s32[]{:S(2)}) async-start(), calls=%async_computation.10 | async-start | bytes 2113536 | tf_op jit(solution)/shard_map/all_gather | solution.py:95
  366.0 23.2 %copy-start.23 = (f32[2,128]{1,0:T(2,128)S(1)}, f32[2,128]{1,0:T(2,128)}, u32[]{:S(2)}) copy-start(f32[2,128]{1,0:T(2,128)} %copy-done.22) | copy-start | bytes 3076
  508.7 33.3 %copy-start.17 = (pred[16,16]{1,0:T(8,128)(4,1)S(1)}, pred[16,16]{1,0:T(8,128)(4,1)}, u32[]{:S(2)}) copy-start(pred[16,16]{1,0:T(8,128)(4,1)} %iota_compare_fusion.9) | copy-start | bytes 772
  508.7 33.4 %copy-start.15 = (pred[16,16]{1,0:T(8,128)(4,1)S(1)}, pred[16,16]{1,0:T(8,128)(4,1)}, u32[]{:S(2)}) copy-start(pred[16,16]{1,0:T(8,128)(4,1)} %iota_compare_fusion.8) | copy-start | bytes 772
  548.5 15.6 %all-to-all-start.5 = ((f32[128,1,256]{2,1,0:T(1,128)}), f32[128,1,256]{2,1,0:T(1,128)}, u32[]{:S(2)}, u32[]{:S(2)}) async-start(f32[128,1,256]{2,1,0:T(1,128)} %copy.332), calls=%async_computation.5 | async-start | bytes 262144 | tf_op jit(solution)/shard_map/all_to_all | solution.py:110
  564.1 23.8 %all-to-all-start.4 = ((f32[128,1,16,128]{3,2,1,0:T(8,128)}), f32[128,1,16,128]{3,2,1,0:T(8,128)}, u32[]{:S(2)}, u32[]{:S(2)}) async-start(f32[128,1,16,128]{3,2,1,0:T(8,128)} %bitcast_multiply_fusion.1), calls=%async_computation.4 | async-start | bytes 2097152 | tf_op jit(solution)/shard_map/all_to_all | solution.py:109
  569.2 22.3 %copy-start.28 = (pred[2,128]{1,0:T(4,128)(4,1)S(1)}, pred[2,128]{1,0:T(4,128)(4,1)}, u32[]{:S(2)}) copy-start(pred[2,128]{1,0:T(4,128)(4,1)} %copy-done.26) | copy-start | bytes 772
  569.3 22.2 %copy-start.33 = (f32[128]{0:T(128)S(1)}, f32[128]{0:T(128)}, u32[]{:S(2)}) copy-start(f32[128]{0:T(128)} %copy-done.31) | copy-start | bytes 1540
  569.3 136.6 %all-gather.11.cloned.1.call-start = ((), (), s32[]{:S(2)}) async-start(), calls=%async_computation.11 | async-start | bytes 2113536 | tf_op jit(solution)/shard_map/all_gather | solution.py:95
  571.8 23.2 %copy-start.24 = (f32[2,128]{1,0:T(2,128)S(1)}, f32[2,128]{1,0:T(2,128)}, u32[]{:S(2)}) copy-start(f32[2,128]{1,0:T(2,128)} %copy-done.22) | copy-start | bytes 3076
  716.2 29.6 %copy-start.18 = (pred[16,16]{1,0:T(8,128)(4,1)S(1)}, pred[16,16]{1,0:T(8,128)(4,1)}, u32[]{:S(2)}) copy-start(pred[16,16]{1,0:T(8,128)(4,1)} %iota_compare_fusion.9) | copy-start | bytes 772
  716.2 29.8 %copy-start.16 = (pred[16,16]{1,0:T(8,128)(4,1)S(1)}, pred[16,16]{1,0:T(8,128)(4,1)}, u32[]{:S(2)}) copy-start(pred[16,16]{1,0:T(8,128)(4,1)} %iota_compare_fusion.8) | copy-start | bytes 772
  751.3 15.3 %all-to-all-start.7 = ((f32[128,1,256]{2,1,0:T(1,128)}), f32[128,1,256]{2,1,0:T(1,128)S(1)}, u32[]{:S(2)}, u32[]{:S(2)}) async-start(f32[128,1,256]{2,1,0:T(1,128)} %copy.356), calls=%async_computation.7 | async-start | bytes 262144 | tf_op jit(solution)/shard_map/all_to_all | solution.py:110
  766.7 23.8 %all-to-all-start.6 = ((f32[128,1,16,128]{3,2,1,0:T(8,128)}), f32[128,1,16,128]{3,2,1,0:T(8,128)}, u32[]{:S(2)}, u32[]{:S(2)}) async-start(f32[128,1,16,128]{3,2,1,0:T(8,128)} %bitcast_multiply_fusion), calls=%async_computation.6 | async-start | bytes 2097152 | tf_op jit(solution)/shard_map/all_to_all | solution.py:109
  772.0 22.1 %copy-start.29 = (pred[2,128]{1,0:T(4,128)(4,1)S(1)}, pred[2,128]{1,0:T(4,128)(4,1)}, u32[]{:S(2)}) copy-start(pred[2,128]{1,0:T(4,128)(4,1)} %copy-done.26) | copy-start | bytes 772
  773.6 24.1 %copy-start.25 = (f32[2,128]{1,0:T(2,128)S(1)}, f32[2,128]{1,0:T(2,128)}, u32[]{:S(2)}) copy-start(f32[2,128]{1,0:T(2,128)} %copy-done.22) | copy-start | bytes 3076
  (17 other events, 182.5 us)
Sparse Core Ops, SparseCore 0:
  11.1 69.1 all-gather.4
  231.1 62.2 all-gather.6
  437.9 62.2 all-gather.8
  643.6 62.2 all-gather.10
where the time goes:
time: 864 us; the launch traced here: 853 us
  other arithmetic  322 us (37%)
  waiting for transfers between devices  275 us (32%)
  local copies, waits for them, and re-layouts  119 us (14%)
  matrix products  72.2 us (8%)
  starting transfers between devices  49.9 us (6%)
  between operations  15.1 us (2%)
    all_gather x4, waiting for transfers between devices, body(): everything = lax.all_gather(precoders, 'cells', axis=0, tiled=True)  188 us
    another operation x39, other arithmetic, spd_solve(): factor = jnp.linalg.cholesky(matrix)  161 us
    another operation x27, other arithmetic, spd_solve(): lax.linalg.triangular_solve(factor, middle, left_side=True, lower=True, t...  135 us
    all_to_all x4, waiting for transfers between devices, body(): lax.all_to_all(outgoing_filters, 'cells', split_axis=0, concat_axis=0, ti...  64.3 us
    gather x5, local copies, waits for them, and re-layouts, link_tables(): positions = inverse[linked]  61.7 us
    all_to_all x4, starting transfers between devices, body(): lax.all_to_all(link_weights.reshape(devices, capacity, streams * streams)...  28.9 us
    all_to_all x4, waiting for transfers between devices, body(): lax.all_to_all(link_weights.reshape(devices, capacity, streams * streams)...  22 us
    dot_general x4, matrix products, receiver_step(): jnp.einsum('klrn,kldn->kldr', channels, link_precoders, precision=HIGHEST)  21.5 us
  transfers between devices with their start and end apart: 12, of which 12 were waited for; matrix products, arithmetic and copies ran while one was open for 12% of the time, Pallas kernels for 0%

commit v1 on v0

--- a/solution.py
+++ b/solution.py
@@ -92,7 +92,9 @@
     precoders = precoders_init
     weights = jnp.zeros((groups, streams, streams), jnp.float32)
     for layer_index in range(LAYERS):
-        everything = lax.all_gather(precoders, "cells", axis=0, tiled=True)
+        everything = jnp.concatenate(
+            lax.all_to_all(jnp.stack([precoders] * lax.axis_size("cells")), "cells", 0, 0), axis=0
+        )
         link_precoders = everything[mine_positions]
         weights, transposed = receiver_step(
             channels, link_precoders.reshape(groups, link_count, streams, antennas), my_in_use

time: 864 us -> 768 us (0.89)
  waiting for transfers between devices: 275 us -> 94.7 us
  blocking collectives: 0 us -> 106 us
  between operations: 15.1 us -> 2.11 us
    all_gather x4 -> x0, waiting for transfers between devices: 188 us -> none  [body(): everything = lax.all_gather(precoders, 'cells', axis=0, tiled=True)]
    all_to_all x0 -> x3, blocking collectives: none -> 106 us  [body(): lax.all_to_all(jnp.stack([precoders] * lax.axis_size('cells')), 'cells',...]
    all_to_all x0 -> x1, starting transfers between devices: none -> 12 us  [body(): lax.all_to_all(jnp.stack([precoders] * lax.axis_size('cells')), 'cells',...]
  transfers between devices with their start and end apart: 12 -> 9, of which waited for: 12 -> 8; matrix products, arithmetic and copies ran while one was open for 12% -> 11% of each run, Pallas kernels for 0% -> 0%
where the time goes in v1:
time: 768 us; the launch traced here: 757 us
  other arithmetic  314 us (41%)
  local copies, waits for them, and re-layouts  115 us (15%)
  blocking collectives  106 us (14%)
  waiting for transfers between devices  94.7 us (12%)
  matrix products  67.5 us (9%)
  starting transfers between devices  57.5 us (7%)
    another operation x39, other arithmetic, spd_solve(): factor = jnp.linalg.cholesky(matrix)  157 us
    another operation x27, other arithmetic, spd_solve(): lax.linalg.triangular_solve(factor, middle, left_side=True, lower=True, t...  134 us
    all_to_all x3, blocking collectives, body(): lax.all_to_all(jnp.stack([precoders] * lax.axis_size('cells')), 'cells',...  106 us
    all_to_all x4, waiting for transfers between devices, body(): lax.all_to_all(outgoing_filters, 'cells', split_axis=0, concat_axis=0, ti...  66 us
    gather x5, local copies, waits for them, and re-layouts, link_tables(): positions = inverse[linked]  61.7 us
    all_to_all x4, waiting for transfers between devices, body(): lax.all_to_all(link_weights.reshape(devices, capacity, streams * streams)...  28.7 us
    all_to_all x4, starting transfers between devices, body(): lax.all_to_all(link_weights.reshape(devices, capacity, streams * streams)...  24.3 us
    dot_general x4, matrix products, receiver_step(): jnp.einsum('klrn,kldn->kldr', channels, link_precoders, precision=HIGHEST)  21.5 us
  transfers between devices with their start and end apart: 9, of which 8 were waited for; matrix products, arithmetic and copies ran while one was open for 11% of the time, Pallas kernels for 0%

profile of v1, /device:TPU:1, one launch (start us, length us, event | category | flops | bytes accessed | tf_op | source)
XLA Modules:
  0.0 756.8 jit_solution(2552601756321907480)
XLA Ops:
  3.1 12.0 %all-to-all-start = ((f32[128,2,16,128]{3,2,1,0:T(8,128)}), f32[128,2,16,128]{3,2,1,0:T(8,128)}, u32[]{:S(2)}, u32[]{:S(2)}) async-start(f32[128,2,16,128]{3,2,1,0:T(8,128)} %stack.8), calls=%async_computation | async-start | bytes 4194304 | tf_op jit(solution)/shard_map/all_to_all | solution.py:96
  18.8 61.3 %gather_fusion = s32[10496]{0:T(1024)S(1)} fusion(s32[256]{0:T(256)S(1)} %get-tuple-element.6, s32[11264]{0:T(1024)S(1)} %pad_clamp_fusion), kind=kCustom, calls=%fused_computation | custom fusion | bytes 125952 | tf_op jit(solution)/shard_map/gather | solution.py:21
  85.6 5.4 broadcast_multiply_fusion.3
  94.9 12.5 %custom-call.54 = f32[2,64,64]{2,1,0:T(8,128)S(1)} custom-call(f32[2,64,64]{2,1,0:T(8,128)} %fusion.99), custom_call_target="Cholesky" | custom-call | tf_op jit(solution)/shard_map/jit(cholesky)/cholesky | solution.py:13
  108.3 10.6 %custom-call.56 = f32[2,1,64,64]{2,3,1,0:T(8,128)S(1)} custom-call(f32[2,1,64,64]{3,2,1,0:T(8,128)} %select_bitcast_fusion.7), custom_call_target="InvertDiagBlocksLowerTriangular" | custom-call | tf_op jit(solution)/shard_map/triangular_solve/custom-call.4 | solution.py:15
  130.9 10.2 %all-to-all-start.2 = ((f32[128,1,256]{2,1,0:T(1,128)}), f32[128,1,256]{2,1,0:T(1,128)}, u32[]{:S(2)}, u32[]{:S(2)}) async-start(f32[128,1,256]{2,1,0:T(1,128)} %copy.284), calls=%async_computation.2 | async-start | bytes 262144 | tf_op jit(solution)/shard_map/all_to_all | solution.py:112
  145.4 5.5 all-to-all-done.2
  159.2 15.5 %all-to-all-done.1 = f32[128,1,16,128]{3,2,1,0:T(8,128)} async-done(((f32[128,1,16,128]{3,2,1,0:T(8,128)}), f32[128,1,16,128]{3,2,1,0:T(8,128)}, u32[]{:S(2)}, u32[]{:S(2)}) %all-to-all-start.1) | async-done | bytes 1048608 | tf_op jit(solution)/shard_map/all_to_all | solution.py:111
  183.3 23.5 %custom-call.60 = f32[2,128,128]{2,1,0:T(8,128)S(1)} custom-call(f32[2,128,128]{2,1,0:T(8,128)S(1)} %fusion.79), custom_call_target="Cholesky" | custom-call | tf_op jit(solution)/shard_map/jit(cholesky)/cholesky | solution.py:13
  207.0 19.7 %custom-call.62 = f32[2,1,128,128]{2,3,1,0:T(8,128)S(1)} custom-call(f32[2,1,128,128]{3,2,1,0:T(8,128)S(1)} %select_bitcast_fusion.3), custom_call_target="InvertDiagBlocksLowerTriangular" | custom-call | tf_op jit(solution)/shard_map/triangular_solve/custom-call.8 | solution.py:15
  229.6 35.2 %all_to_all.60 = f32[128,2,16,128]{3,2,1,0:T(8,128)} all-to-all(f32[128,2,16,128]{3,2,1,0:T(8,128)S(1)} %stack.9), channel_id=1, replica_groups=mesh['cells'=128] {'cells'}, dimensions={0} | all-to-all | bytes 4194304 | tf_op jit(solution)/shard_map/all_to_all | solution.py:96
  277.3 12.5 %custom-call.63 = f32[2,64,64]{2,1,0:T(8,128)S(1)} custom-call(f32[2,64,64]{2,1,0:T(8,128)} %fusion.94), custom_call_target="Cholesky" | custom-call | tf_op jit(solution)/shard_map/jit(cholesky)/cholesky | solution.py:13
  290.6 10.6 %custom-call.65 = f32[2,1,64,64]{2,3,1,0:T(8,128)S(1)} custom-call(f32[2,1,64,64]{3,2,1,0:T(8,128)} %select_bitcast_fusion.6), custom_call_target="InvertDiagBlocksLowerTriangular" | custom-call | tf_op jit(solution)/shard_map/triangular_solve/custom-call.4 | solution.py:15
  320.8 7.7 %all-to-all-done.5 = f32[128,1,256]{2,1,0:T(1,128)S(1)} async-done(((f32[128,1,256]{2,1,0:T(1,128)}), f32[128,1,256]{2,1,0:T(1,128)S(1)}, u32[]{:S(2)}, u32[]{:S(2)}) %all-to-all-start.5) | async-done | bytes 131104 | tf_op jit(solution)/shard_map/all_to_all | solution.py:112
  335.4 16.8 %all-to-all-done.4 = f32[128,1,16,128]{3,2,1,0:T(8,128)} async-done(((f32[128,1,16,128]{3,2,1,0:T(8,128)}), f32[128,1,16,128]{3,2,1,0:T(8,128)}, u32[]{:S(2)}, u32[]{:S(2)}) %all-to-all-start.4) | async-done | bytes 1048608 | tf_op jit(solution)/shard_map/all_to_all | solution.py:111
  360.7 23.5 %custom-call.69 = f32[2,128,128]{2,1,0:T(8,128)S(1)} custom-call(f32[2,128,128]{2,1,0:T(8,128)S(1)} %fusion.75), custom_call_target="Cholesky" | custom-call | tf_op jit(solution)/shard_map/jit(cholesky)/cholesky | solution.py:13
  384.5 19.7 %custom-call.71 = f32[2,1,128,128]{2,3,1,0:T(8,128)S(1)} custom-call(f32[2,1,128,128]{3,2,1,0:T(8,128)S(1)} %select_bitcast_fusion.2), custom_call_target="InvertDiagBlocksLowerTriangular" | custom-call | tf_op jit(solution)/shard_map/triangular_solve/custom-call.8 | solution.py:15
  405.0 35.4 %all_to_all.61 = f32[128,2,16,128]{3,2,1,0:T(8,128)} all-to-all(f32[128,2,16,128]{3,2,1,0:T(8,128)S(1)} %stack.10), channel_id=1, replica_groups=mesh['cells'=128] {'cells'}, dimensions={0} | all-to-all | bytes 4194304 | tf_op jit(solution)/shard_map/all_to_all | solution.py:96
  452.9 12.5 %custom-call.72 = f32[2,64,64]{2,1,0:T(8,128)S(1)} custom-call(f32[2,64,64]{2,1,0:T(8,128)} %fusion.89), custom_call_target="Cholesky" | custom-call | tf_op jit(solution)/shard_map/jit(cholesky)/cholesky | solution.py:13
  466.2 10.6 %custom-call.74 = f32[2,1,64,64]{2,3,1,0:T(8,128)S(1)} custom-call(f32[2,1,64,64]{3,2,1,0:T(8,128)} %select_bitcast_fusion.5), custom_call_target="InvertDiagBlocksLowerTriangular" | custom-call | tf_op jit(solution)/shard_map/triangular_solve/custom-call.4 | solution.py:15
  496.4 7.7 %all-to-all-done.8 = f32[128,1,256]{2,1,0:T(1,128)S(1)} async-done(((f32[128,1,256]{2,1,0:T(1,128)}), f32[128,1,256]{2,1,0:T(1,128)S(1)}, u32[]{:S(2)}, u32[]{:S(2)}) %all-to-all-start.8) | async-done | bytes 131104 | tf_op jit(solution)/shard_map/all_to_all | solution.py:112
  511.0 16.8 %all-to-all-done.7 = f32[128,1,16,128]{3,2,1,0:T(8,128)} async-done(((f32[128,1,16,128]{3,2,1,0:T(8,128)}), f32[128,1,16,128]{3,2,1,0:T(8,128)}, u32[]{:S(2)}, u32[]{:S(2)}) %all-to-all-start.7) | async-done | bytes 1048608 | tf_op jit(solution)/shard_map/all_to_all | solution.py:111
  536.3 23.5 %custom-call.78 = f32[2,128,128]{2,1,0:T(8,128)S(1)} custom-call(f32[2,128,128]{2,1,0:T(8,128)S(1)} %fusion.71), custom_call_target="Cholesky" | custom-call | tf_op jit(solution)/shard_map/jit(cholesky)/cholesky | solution.py:13
  560.0 19.7 %custom-call.80 = f32[2,1,128,128]{2,3,1,0:T(8,128)S(1)} custom-call(f32[2,1,128,128]{3,2,1,0:T(8,128)S(1)} %select_bitcast_fusion.1), custom_call_target="InvertDiagBlocksLowerTriangular" | custom-call | tf_op jit(solution)/shard_map/triangular_solve/custom-call.8 | solution.py:15
  580.5 35.2 %all_to_all.62 = f32[128,2,16,128]{3,2,1,0:T(8,128)} all-to-all(f32[128,2,16,128]{3,2,1,0:T(8,128)S(1)} %stack.11), channel_id=1, replica_groups=mesh['cells'=128] {'cells'}, dimensions={0} | all-to-all | bytes 4194304 | tf_op jit(solution)/shard_map/all_to_all | solution.py:96
  628.2 12.5 %custom-call.81 = f32[2,64,64]{2,1,0:T(8,128)S(1)} custom-call(f32[2,64,64]{2,1,0:T(8,128)} %fusion.84), custom_call_target="Cholesky" | custom-call | tf_op jit(solution)/shard_map/jit(cholesky)/cholesky | solution.py:13
  641.6 10.6 %custom-call.83 = f32[2,1,64,64]{2,3,1,0:T(8,128)S(1)} custom-call(f32[2,1,64,64]{3,2,1,0:T(8,128)} %select_bitcast_fusion.4), custom_call_target="InvertDiagBlocksLowerTriangular" | custom-call | tf_op jit(solution)/shard_map/triangular_solve/custom-call.4 | solution.py:15
  671.8 7.7 %all-to-all-done.11 = f32[128,1,256]{2,1,0:T(1,128)S(1)} async-done(((f32[128,1,256]{2,1,0:T(1,128)}), f32[128,1,256]{2,1,0:T(1,128)S(1)}, u32[]{:S(2)}, u32[]{:S(2)}) %all-to-all-start.11) | async-done | bytes 131104 | tf_op jit(solution)/shard_map/all_to_all | solution.py:112
  679.5 5.4 all-to-all-start.10
  686.4 16.9 %all-to-all-done.10 = f32[128,1,16,128]{3,2,1,0:T(8,128)} async-done(((f32[128,1,16,128]{3,2,1,0:T(8,128)}), f32[128,1,16,128]{3,2,1,0:T(8,128)}, u32[]{:S(2)}, u32[]{:S(2)}) %all-to-all-start.10) | async-done | bytes 1048608 | tf_op jit(solution)/shard_map/all_to_all | solution.py:111
  711.8 23.5 %custom-call.87 = f32[2,128,128]{2,1,0:T(8,128)S(1)} custom-call(f32[2,128,128]{2,1,0:T(8,128)S(1)} %fusion.67), custom_call_target="Cholesky" | custom-call | tf_op jit(solution)/shard_map/jit(cholesky)/cholesky | solution.py:13
  735.6 19.7 %custom-call.89 = f32[2,1,128,128]{2,3,1,0:T(8,128)S(1)} custom-call(f32[2,1,128,128]{3,2,1,0:T(8,128)S(1)} %select_bitcast_fusion), custom_call_target="InvertDiagBlocksLowerTriangular" | custom-call | tf_op jit(solution)/shard_map/triangular_solve/custom-call.8 | solution.py:15
  (275 shorter events, 195.2 us)
Async XLA Ops:
  0.6 85.0 %copy-start = (f32[2,41,64,128]{3,2,1,0:T(8,128)S(1)}, f32[2,41,64,128]{3,2,1,0:T(8,128)}, u32[]{:S(2)}) copy-start(f32[2,41,64,128]{3,2,1,0:T(8,128)} %param.21) | copy-start | bytes 8060932
  3.1 12.0 %copy-start.24 = (s32[256]{0:T(256)S(1)}, s32[256]{0:T(256)}, u32[]{:S(2)}) copy-start(s32[256]{0:T(256)} %param.26) | copy-start | bytes 3076
  3.1 12.1 %copy-start.14 = (s32[256,40]{0,1:T(8,128)S(1)}, s32[256,40]{0,1:T(8,128)}, u32[]{:S(2)}) copy-start(s32[256,40]{0,1:T(8,128)} %param.25) | copy-start | bytes 122884
  3.1 12.1 %copy-start.25 = (s32[256]{0:T(256)S(1)}, s32[256]{0:T(256)}, u32[]{:S(2)}) copy-start(s32[256]{0:T(256)} %param.23) | copy-start | bytes 3076
  3.1 12.5 %copy-start.26 = (s32[256]{0:T(256)S(1)}, s32[256]{0:T(256)}, u32[]{:S(2)}) copy-start(s32[256]{0:T(256)} %param.24) | copy-start | bytes 3076
  3.1 79.5 %all-to-all-start = ((f32[128,2,16,128]{3,2,1,0:T(8,128)}), f32[128,2,16,128]{3,2,1,0:T(8,128)}, u32[]{:S(2)}, u32[]{:S(2)}) async-start(f32[128,2,16,128]{3,2,1,0:T(8,128)} %stack.8), calls=%async_computation | async-start | bytes 4194304 | tf_op jit(solution)/shard_map/all_to_all | solution.py:96
  80.3 5.3 copy-start.11
  80.5 5.2 copy-start.22
  82.3 8.7 %copy-start.15 = (s32[1024]{0:T(1024)}, s32[1024]{0:T(1024)S(1)}, u32[]{:S(2)}) copy-start(s32[1024]{0:T(1024)S(1)} %pad_clamp_fusion.3) | copy-start | bytes 12292
  82.5 45.2 %copy-start.16 = (s32[1024]{0:T(1024)}, s32[1024]{0:T(1024)S(1)}, u32[]{:S(2)}) copy-start(s32[1024]{0:T(1024)S(1)} %get-tuple-element.31) | copy-start | bytes 12292
  82.5 58.6 %copy-start.17 = (s32[1024]{0:T(1024)}, s32[1024]{0:T(1024)S(1)}, u32[]{:S(2)}) copy-start(s32[1024]{0:T(1024)S(1)} %get-tuple-element.32) | copy-start | bytes 12292
  91.0 28.0 %copy-start.8 = (f32[2,41,16,64]{3,2,1,0:T(8,128)}, f32[2,41,16,64]{3,2,1,0:T(8,128)S(1)}, u32[]{:S(2)}) copy-start(f32[2,41,16,64]{3,2,1,0:T(8,128)S(1)} %get-tuple-element.24) | copy-start | bytes 1007620
  130.9 20.0 %all-to-all-start.2 = ((f32[128,1,256]{2,1,0:T(1,128)}), f32[128,1,256]{2,1,0:T(1,128)}, u32[]{:S(2)}, u32[]{:S(2)}) async-start(f32[128,1,256]{2,1,0:T(1,128)} %copy.284), calls=%async_computation.2 | async-start | bytes 262144 | tf_op jit(solution)/shard_map/all_to_all | solution.py:112
  142.9 13.3 %copy-start.12 = (s32[128,2,41]{0,2,1:T(8,128)S(1)}, s32[128,2,41]{0,2,1:T(8,128)}, u32[]{:S(2)}) copy-start(s32[128,2,41]{0,2,1:T(8,128)} %copy-done.11) | copy-start | bytes 125956
  142.9 13.5 %copy-start.13 = (s32[128,82]{0,1:T(8,128)S(1)}, s32[128,82]{0,1:T(8,128)}, u32[]{:S(2)}) copy-start(s32[128,82]{0,1:T(8,128)} %get-tuple-element.19) | copy-start | bytes 125956
  142.9 13.6 %copy-start.23 = (s32[82]{0:T(128)S(1)}, s32[82]{0:T(128)}, u32[]{:S(2)}) copy-start(s32[82]{0:T(128)} %copy-done.22) | copy-start | bytes 988
  150.9 23.8 %all-to-all-start.1 = ((f32[128,1,16,128]{3,2,1,0:T(8,128)}), f32[128,1,16,128]{3,2,1,0:T(8,128)}, u32[]{:S(2)}, u32[]{:S(2)}) async-start(f32[128,1,16,128]{3,2,1,0:T(8,128)} %bitcast_multiply_fusion.3), calls=%async_computation.1 | async-start | bytes 2097152 | tf_op jit(solution)/shard_map/all_to_all | solution.py:111
  156.7 70.0 %copy-start.18 = (f32[128]{0:T(128)}, f32[128]{0:T(128)S(1)}, u32[]{:S(2)}) copy-start(f32[128]{0:T(128)S(1)} %convert_element_type.98) | copy-start | bytes 1540
  177.3 3.8 copy-start.6
  273.3 28.0 %copy-start.9 = (f32[2,41,16,64]{3,2,1,0:T(8,128)}, f32[2,41,16,64]{3,2,1,0:T(8,128)S(1)}, u32[]{:S(2)}) copy-start(f32[2,41,16,64]{3,2,1,0:T(8,128)S(1)} %get-tuple-element.26) | copy-start | bytes 1007620
  313.6 14.9 %all-to-all-start.5 = ((f32[128,1,256]{2,1,0:T(1,128)}), f32[128,1,256]{2,1,0:T(1,128)S(1)}, u32[]{:S(2)}, u32[]{:S(2)}) async-start(f32[128,1,256]{2,1,0:T(1,128)} %copy.308), calls=%async_computation.5 | async-start | bytes 262144 | tf_op jit(solution)/shard_map/all_to_all | solution.py:112
  328.5 23.8 %all-to-all-start.4 = ((f32[128,1,16,128]{3,2,1,0:T(8,128)}), f32[128,1,16,128]{3,2,1,0:T(8,128)}, u32[]{:S(2)}, u32[]{:S(2)}) async-start(f32[128,1,16,128]{3,2,1,0:T(8,128)} %bitcast_multiply_fusion.2), calls=%async_computation.4 | async-start | bytes 2097152 | tf_op jit(solution)/shard_map/all_to_all | solution.py:111
  354.9 3.7 copy-start.4
  448.9 28.0 %copy-start.10 = (f32[2,41,16,64]{3,2,1,0:T(8,128)}, f32[2,41,16,64]{3,2,1,0:T(8,128)S(1)}, u32[]{:S(2)}) copy-start(f32[2,41,16,64]{3,2,1,0:T(8,128)S(1)} %get-tuple-element.28) | copy-start | bytes 1007620
  489.2 14.9 %all-to-all-start.8 = ((f32[128,1,256]{2,1,0:T(1,128)}), f32[128,1,256]{2,1,0:T(1,128)S(1)}, u32[]{:S(2)}, u32[]{:S(2)}) async-start(f32[128,1,256]{2,1,0:T(1,128)} %copy.332), calls=%async_computation.8 | async-start | bytes 262144 | tf_op jit(solution)/shard_map/all_to_all | solution.py:112
  504.1 23.7 %all-to-all-start.7 = ((f32[128,1,16,128]{3,2,1,0:T(8,128)}), f32[128,1,16,128]{3,2,1,0:T(8,128)}, u32[]{:S(2)}, u32[]{:S(2)}) async-start(f32[128,1,16,128]{3,2,1,0:T(8,128)} %bitcast_multiply_fusion.1), calls=%async_computation.7 | async-start | bytes 2097152 | tf_op jit(solution)/shard_map/all_to_all | solution.py:111
  530.4 3.7 copy-start.5
  624.3 28.0 %copy-start.7 = (f32[2,41,16,64]{3,2,1,0:T(8,128)}, f32[2,41,16,64]{3,2,1,0:T(8,128)S(1)}, u32[]{:S(2)}) copy-start(f32[2,41,16,64]{3,2,1,0:T(8,128)S(1)} %get-tuple-element.30) | copy-start | bytes 1007620
  662.9 16.6 %copy-start.1 = (f32[2,256]{1,0:T(2,128)}, f32[2,256]{1,0:T(2,128)S(1)}, u32[]{:S(2)}) copy-start(f32[2,256]{1,0:T(2,128)S(1)} %reshape.867) | copy-start | bytes 6148
  664.7 14.9 %all-to-all-start.11 = ((f32[128,1,256]{2,1,0:T(1,128)}), f32[128,1,256]{2,1,0:T(1,128)S(1)}, u32[]{:S(2)}, u32[]{:S(2)}) async-start(f32[128,1,256]{2,1,0:T(1,128)} %copy.356), calls=%async_computation.11 | async-start | bytes 262144 | tf_op jit(solution)/shard_map/all_to_all | solution.py:112
  679.5 23.8 %all-to-all-start.10 = ((f32[128,1,16,128]{3,2,1,0:T(8,128)}), f32[128,1,16,128]{3,2,1,0:T(8,128)}, u32[]{:S(2)}, u32[]{:S(2)}) async-start(f32[128,1,16,128]{3,2,1,0:T(8,128)} %bitcast_multiply_fusion), calls=%async_computation.10 | async-start | bytes 2097152 | tf_op jit(solution)/shard_map/all_to_all | solution.py:111
  706.0 3.7 copy-start.3
  (4 other events, 9.4 us)
